TPU v7x, 32 devices: a whole 2x2x4 slice. The times are simulated.
32 devices in a mesh: conv: 2 (over y), ctx: 4 (over x, core), head: 4 (over z).
Axes of the slice: x: 2, y: 2, z: 4, core: 2. Of those that a mesh axis runs over, the one named last changes fastest.
Arguments:
- queries: bfloat16 [512, 64, 128], P(('conv', 'ctx'), 'head'), parts along dimension 0, may hold values from -240 to 240, as said below
- new_keys: bfloat16 [512, 8, 128], P(('conv', 'ctx'), 'head'), parts along dimension 0, may hold values from -8 to 8
- new_values: bfloat16 [512, 8, 128], P(('conv', 'ctx'), 'head'), parts along dimension 0, may hold values from -18 to 18
- cache_keys: bfloat16 [16384, 8, 128], P(('conv', 'ctx'), 'head'), parts along dimension 0, may hold values from -6 to 6
- cache_values: bfloat16 [16384, 8, 128], P(('conv', 'ctx'), 'head'), parts along dimension 0, may hold values from -18 to 18
- cache_len: int32 [2], P('conv'), parts along dimension 0, may hold values from 4097 to 8192
Outputs:
- attended: bfloat16 [512, 64, 128], P(('conv', 'ctx'), 'head'), parts along dimension 0
There are 2 independent parts, one for each index of `conv`. A program takes and returns all parts, laid end to end along the dimension named above; each array names one. Nothing has to cross between parts.
Inputs may be any that keep to these rules, and one draw needn't show every extreme that they name: `queries`: each query row is a row of independent entries times a row scale.
All inputs are finite; a program needn't handle non-finite values.
Results may differ from a plain program's by a relative error of at most 0.01.
Values may be sent and summed in bfloat16 or wider, within the bound.
A program may use at most 64 MiB of HBM per device.

v0:
```python
import math
import jax
import jax.numpy as jnp
from jax import lax
from jax.sharding import PartitionSpec as P

NEG_FILL = -1e30


def attend_block(query_rows, keys, values, valid):
    scores = jnp.einsum("tkgd,skd->tkgs", query_rows, keys, preferred_element_type=jnp.float32) * (
        1.0 / math.sqrt(keys.shape[-1])
    )
    mask = valid[:, None, None, :]
    scores = jnp.where(mask, scores, NEG_FILL)
    peak = jnp.max(scores, axis=-1)
    expo = jnp.where(mask, jnp.exp(scores - peak[..., None]), 0.0)
    total = jnp.sum(expo, axis=-1)
    out = jnp.einsum(
        "tkgs,skd->tkgd", expo.astype(jnp.bfloat16), values, preferred_element_type=jnp.float32
    )
    return (out, peak, total)


def per_device(queries, new_keys, new_values, cache_keys, cache_values, cache_len):
    q_rows, heads_local, head_size = queries.shape
    slots, kv_local, _ = cache_keys.shape
    group = heads_local // kv_local
    place = lax.axis_index("ctx")
    limit = cache_len[0]
    slot_valid = place * slots + lax.iota(jnp.int32, slots) < limit
    piece = lax.all_gather(queries, "ctx", axis=0, tiled=True)
    rows = piece.shape[0]
    block = math.gcd(rows, 64)
    blocks = piece.reshape(rows // block, block, kv_local, group, head_size)

    def one_block(blk):
        out, peak, total = attend_block(blk, cache_keys, cache_values, slot_valid[None, :])
        floored = jnp.maximum(total, 1.0)
        norm = (out / floored[..., None]).astype(jnp.bfloat16)
        lse = peak + jnp.log(floored)
        return (norm.reshape(block, heads_local, head_size), lse.reshape(block, heads_local))

    norm, lse = lax.map(one_block, blocks)
    norm, lse = (norm.reshape(rows, heads_local, head_size), lse.reshape(rows, heads_local))
    turn_k, turn_v = (
        lax.all_gather(new_keys, "ctx", axis=0, tiled=True),
        lax.all_gather(new_values, "ctx", axis=0, tiled=True),
    )
    own_ids = place * q_rows + lax.iota(jnp.int32, q_rows)
    causal = lax.iota(jnp.int32, turn_k.shape[0])[None, :] <= own_ids[:, None]
    turn_out, turn_max, turn_total = attend_block(
        queries.reshape(q_rows, kv_local, group, head_size), turn_k, turn_v, causal
    )
    turn_out = turn_out.reshape(q_rows, heads_local, head_size)
    turn_max = turn_max.reshape(q_rows, heads_local)
    turn_total = turn_total.reshape(q_rows, heads_local)
    got_norm = lax.all_to_all(norm[None], "ctx", split_axis=1, concat_axis=0, tiled=True)
    got_lse = lax.all_to_all(lse[None], "ctx", split_axis=1, concat_axis=0, tiled=True)
    top = jnp.maximum(jnp.max(got_lse, axis=0), turn_max)
    shard_scale = jnp.exp(got_lse - top[None])
    numer = jnp.einsum("sthd,sth->thd", got_norm.astype(jnp.float32), shard_scale)
    denom = jnp.sum(shard_scale, axis=0)
    turn_scale = jnp.exp(turn_max - top)
    numer = numer + turn_out * turn_scale[..., None]
    denom = denom + turn_total * turn_scale
    return (numer / denom[..., None]).astype(jnp.bfloat16)


def solution(mesh):
    return jax.shard_map(
        per_device,
        mesh=mesh,
        in_specs=(
            P(("conv", "ctx"), "head", None),
            P(("conv", "ctx"), "head", None),
            P(("conv", "ctx"), "head", None),
            P(("conv", "ctx"), "head", None),
            P(("conv", "ctx"), "head", None),
            P("conv"),
        ),
        out_specs=P(("conv", "ctx"), "head", None),
        check_vma=False,
    )
```

profile of v0, /device:TPU:0, one launch (start us, length us, event | category | flops | bytes accessed | tf_op | source)
XLA Modules:
  0.0 124.3 jit_solution(1532145493059581780)
XLA Ops:
  6.5 0.7 all-gather.2.cloned.1.call-update
  7.3 1.4 %copy.96 = bf16[2048,2,128]{2,0,1:T(8,128)(2,1)S(1)} copy(bf16[2048,2,128]{2,1,0:T(2,128)(2,1)} %param.11) | data formatting | bytes 2097152
  8.7 1.4 %copy.97 = bf16[2048,2,128]{2,0,1:T(8,128)(2,1)S(1)} copy(bf16[2048,2,128]{2,1,0:T(2,128)(2,1)} %param.12) | data formatting | bytes 2097152
  10.0 0.8 copy.100
  10.8 0.8 copy.104
  11.5 6.5 %all_gather.10 = bf16[256,2,128]{2,0,1:T(8,128)(2,1)S(1)} all-gather(bf16[64,2,128]{2,0,1:T(8,128)(2,1)S(1)} %copy.100), channel_id=1, replica_groups=mesh['conv'=2,'ctx'=4,'head'=4] {'ctx'}, dimensions={0}, use_global_device_ids=true | all-gather | bytes 163840 | tf_op jit(solution)/shard_map/all_gather | solution.py:47
  18.0 6.3 %all_gather.11 = bf16[256,2,128]{2,0,1:T(8,128)(2,1)S(1)} all-gather(bf16[64,2,128]{2,0,1:T(8,128)(2,1)S(1)} %copy.104), channel_id=1, replica_groups=mesh['conv'=2,'ctx'=4,'head'=4] {'ctx'}, dimensions={0}, use_global_device_ids=true | all-gather | bytes 163840 | tf_op jit(solution)/shard_map/all_gather | solution.py:48
  24.4 1.3 %fusion.47 = (f32[64,2,8]{0,2,1:T(8,128)S(1)}, f32[64,2,8,256]{3,0,2,1:T(8,128)S(1)}) fusion(bf16[64,2,8,128]{3,2,1,0:T(8,128)(2,1)} %bitcast.124, bf16[256,2,128]{2,0,1:T(8,128)(2,1)S(1)} %all_gather.10, pred[64,256]{1,0:T(8,128)(4,1)S(1)} %iota_compare_fusion), kind=kOutput, calls=%fused_computation.53 | convolution fusion | flops 67894272 | bytes 1462272 | tf_op jit(solution)/shard_map/tkgd,skd->tkgs/dot_general | solution.py:11
  25.8 0.4 fusion.33
  26.2 2.8 %all-gather.2.cloned.1.call-done = bf16[256,16,128]{2,1,0:T(8,128)(2,1)} async-done(((bf16[64,16,128]{2,1,0:T(8,128)(2,1)}), bf16[256,16,128]{2,1,0:T(8,128)(2,1)}) %all-gather.2.cloned.1.call-update) | async-done | bytes 1048592 | tf_op jit(solution)/shard_map/all_gather | solution.py:32
  29.0 58.6 %while.13 = (s32[]{:T(128)}, bf16[4,64,16,128]{3,2,1,0:T(8,128)(2,1)}, f32[4,64,16]{1,2,0:T(8,128)S(1)}, bf16[4,64,2,8,128]{4,3,2,1,0:T(8,128)(2,1)}, bf16[2048,...) while((s32[]{:T(128)}, ...), condition=%wide.region_3.4_spmd.clone, body=%wide.region_0.3_spmd.clone.sunk | while | flops 1101272064 | bytes 61953156 | solution.py:44
  29.0 0.7 add_compare_fusion.2
  29.7 2.4 %bitcast_reduce_fusion.2 = (f32[64,2,8]{2,0,1:T(8,128)S(1)}, f32[2,64,8,2048]{3,2,1,0:T(8,128)S(1)}) fusion(pred[2048]{0:T(1024)(128)(4,1)S(1)} %add_compare_fusion.2, bf16[2048,2,128]{2,0,1:T(8,128)(2,1)S(1)} %get-tuple-element.220, bf16[4,64,2,8,128]{4,3,2,1,0:T(8,128)(2,1)} %get-tuple-element.219, s32[]{:T(128)} %get-tuple-element.207), kind=kOutput, calls=%fused_computation.2.clone.1 | convolution fusion | flops 543161344 | bytes 9705984 | tf_op jit(solution)/shard_map/while/body/eval_jaxpr/tkgd,skd->tkgs/dot_general | solution.py:11
  32.1 3.2 %copy-done = f32[2,64,8,2048]{3,2,1,0:T(8,128)} copy-done((f32[2,64,8,2048]{3,2,1,0:T(8,128)}, f32[2,64,8,2048]{3,2,1,0:T(8,128)S(1)}, u32[]{:S(2)}) %copy-start) | copy-done | bytes 8388632 | tf_op jit(solution)/shard_map/while
  35.4 2.2 %fusion.55 = f32[64,2,8]{2,0,1:T(8,128)S(1)} fusion(f32[2,64,8,2048]{3,2,1,0:T(8,128)S(1)} %get-tuple-element.196, f32[64,2,8]{2,0,1:T(8,128)S(1)} %get-tuple-element.197, pred[2048]{0:T(1024)(128)(4,1)S(1)} %add_compare_fusion.2), kind=kLoop, calls=%fused_computation.6.clone.1 | loop fusion | flops 10484736 | bytes 8398848 | tf_op jit(solution)/shard_map/while/body/eval_jaxpr/reduce_sum | solution.py:18
  37.8 5.1 %fusion.56 = bf16[64,2,8,128]{3,2,0,1:T(8,128)(2,1)S(1)} fusion(bf16[2048,2,128]{2,0,1:T(8,128)(2,1)S(1)} %get-tuple-element.221, f32[2,64,8,2048]{3,2,1,0:T(8,128)} %copy-done, f32[64,2,8]{2,0,1:T(8,128)S(1)} %get-tuple-element.197, pred[2048]{0:T(1024)(128)(4,1)S(1)} %add_compare_fusion.2, f32[64,2,8]{2,0,1:T(8,128)S(1)} %copy.142), kind=kOutput, calls=%fused_computation.16.clone.1 | convolution fusion | flops 547618816 | bytes 9709568 | tf_op jit(solution)/shard_map/while/body/eval_jaxpr/tkgs,skd->tkgd/dot_general | solution.py:19
  42.9 0.8 bitcast_dynamic-update-slice_fusion.4
  43.7 0.7 add_compare_fusion.2
  44.3 2.4 %bitcast_reduce_fusion.2 = (f32[64,2,8]{2,0,1:T(8,128)S(1)}, f32[2,64,8,2048]{3,2,1,0:T(8,128)S(1)}) fusion(pred[2048]{0:T(1024)(128)(4,1)S(1)} %add_compare_fusion.2, bf16[2048,2,128]{2,0,1:T(8,128)(2,1)S(1)} %get-tuple-element.220, bf16[4,64,2,8,128]{4,3,2,1,0:T(8,128)(2,1)} %get-tuple-element.219, s32[]{:T(128)} %get-tuple-element.207), kind=kOutput, calls=%fused_computation.2.clone.1 | convolution fusion | flops 543161344 | bytes 9705984 | tf_op jit(solution)/shard_map/while/body/eval_jaxpr/tkgd,skd->tkgs/dot_general | solution.py:11
  46.8 3.2 %copy-done = f32[2,64,8,2048]{3,2,1,0:T(8,128)} copy-done((f32[2,64,8,2048]{3,2,1,0:T(8,128)}, f32[2,64,8,2048]{3,2,1,0:T(8,128)S(1)}, u32[]{:S(2)}) %copy-start) | copy-done | bytes 8388632 | tf_op jit(solution)/shard_map/while
  50.0 2.2 %fusion.55 = f32[64,2,8]{2,0,1:T(8,128)S(1)} fusion(f32[2,64,8,2048]{3,2,1,0:T(8,128)S(1)} %get-tuple-element.196, f32[64,2,8]{2,0,1:T(8,128)S(1)} %get-tuple-element.197, pred[2048]{0:T(1024)(128)(4,1)S(1)} %add_compare_fusion.2), kind=kLoop, calls=%fused_computation.6.clone.1 | loop fusion | flops 10484736 | bytes 8398848 | tf_op jit(solution)/shard_map/while/body/eval_jaxpr/reduce_sum | solution.py:18
  52.5 5.1 %fusion.56 = bf16[64,2,8,128]{3,2,0,1:T(8,128)(2,1)S(1)} fusion(bf16[2048,2,128]{2,0,1:T(8,128)(2,1)S(1)} %get-tuple-element.221, f32[2,64,8,2048]{3,2,1,0:T(8,128)} %copy-done, f32[64,2,8]{2,0,1:T(8,128)S(1)} %get-tuple-element.197, pred[2048]{0:T(1024)(128)(4,1)S(1)} %add_compare_fusion.2, f32[64,2,8]{2,0,1:T(8,128)S(1)} %copy.142), kind=kOutput, calls=%fused_computation.16.clone.1 | convolution fusion | flops 547618816 | bytes 9709568 | tf_op jit(solution)/shard_map/while/body/eval_jaxpr/tkgs,skd->tkgd/dot_general | solution.py:19
  57.6 0.8 bitcast_dynamic-update-slice_fusion.4
  58.3 0.7 add_compare_fusion.2
  59.0 2.4 %bitcast_reduce_fusion.2 = (f32[64,2,8]{2,0,1:T(8,128)S(1)}, f32[2,64,8,2048]{3,2,1,0:T(8,128)S(1)}) fusion(pred[2048]{0:T(1024)(128)(4,1)S(1)} %add_compare_fusion.2, bf16[2048,2,128]{2,0,1:T(8,128)(2,1)S(1)} %get-tuple-element.220, bf16[4,64,2,8,128]{4,3,2,1,0:T(8,128)(2,1)} %get-tuple-element.219, s32[]{:T(128)} %get-tuple-element.207), kind=kOutput, calls=%fused_computation.2.clone.1 | convolution fusion | flops 543161344 | bytes 9705984 | tf_op jit(solution)/shard_map/while/body/eval_jaxpr/tkgd,skd->tkgs/dot_general | solution.py:11
  61.4 3.2 %copy-done = f32[2,64,8,2048]{3,2,1,0:T(8,128)} copy-done((f32[2,64,8,2048]{3,2,1,0:T(8,128)}, f32[2,64,8,2048]{3,2,1,0:T(8,128)S(1)}, u32[]{:S(2)}) %copy-start) | copy-done | bytes 8388632 | tf_op jit(solution)/shard_map/while
  64.7 2.2 %fusion.55 = f32[64,2,8]{2,0,1:T(8,128)S(1)} fusion(f32[2,64,8,2048]{3,2,1,0:T(8,128)S(1)} %get-tuple-element.196, f32[64,2,8]{2,0,1:T(8,128)S(1)} %get-tuple-element.197, pred[2048]{0:T(1024)(128)(4,1)S(1)} %add_compare_fusion.2), kind=kLoop, calls=%fused_computation.6.clone.1 | loop fusion | flops 10484736 | bytes 8398848 | tf_op jit(solution)/shard_map/while/body/eval_jaxpr/reduce_sum | solution.py:18
  67.1 5.1 %fusion.56 = bf16[64,2,8,128]{3,2,0,1:T(8,128)(2,1)S(1)} fusion(bf16[2048,2,128]{2,0,1:T(8,128)(2,1)S(1)} %get-tuple-element.221, f32[2,64,8,2048]{3,2,1,0:T(8,128)} %copy-done, f32[64,2,8]{2,0,1:T(8,128)S(1)} %get-tuple-element.197, pred[2048]{0:T(1024)(128)(4,1)S(1)} %add_compare_fusion.2, f32[64,2,8]{2,0,1:T(8,128)S(1)} %copy.142), kind=kOutput, calls=%fused_computation.16.clone.1 | convolution fusion | flops 547618816 | bytes 9709568 | tf_op jit(solution)/shard_map/while/body/eval_jaxpr/tkgs,skd->tkgd/dot_general | solution.py:19
  72.2 0.8 bitcast_dynamic-update-slice_fusion.4
  73.0 0.7 add_compare_fusion.2
  73.7 2.4 %bitcast_reduce_fusion.2 = (f32[64,2,8]{2,0,1:T(8,128)S(1)}, f32[2,64,8,2048]{3,2,1,0:T(8,128)S(1)}) fusion(pred[2048]{0:T(1024)(128)(4,1)S(1)} %add_compare_fusion.2, bf16[2048,2,128]{2,0,1:T(8,128)(2,1)S(1)} %get-tuple-element.220, bf16[4,64,2,8,128]{4,3,2,1,0:T(8,128)(2,1)} %get-tuple-element.219, s32[]{:T(128)} %get-tuple-element.207), kind=kOutput, calls=%fused_computation.2.clone.1 | convolution fusion | flops 543161344 | bytes 9705984 | tf_op jit(solution)/shard_map/while/body/eval_jaxpr/tkgd,skd->tkgs/dot_general | solution.py:11
  76.1 3.2 %copy-done = f32[2,64,8,2048]{3,2,1,0:T(8,128)} copy-done((f32[2,64,8,2048]{3,2,1,0:T(8,128)}, f32[2,64,8,2048]{3,2,1,0:T(8,128)S(1)}, u32[]{:S(2)}) %copy-start) | copy-done | bytes 8388632 | tf_op jit(solution)/shard_map/while
  79.3 2.2 %fusion.55 = f32[64,2,8]{2,0,1:T(8,128)S(1)} fusion(f32[2,64,8,2048]{3,2,1,0:T(8,128)S(1)} %get-tuple-element.196, f32[64,2,8]{2,0,1:T(8,128)S(1)} %get-tuple-element.197, pred[2048]{0:T(1024)(128)(4,1)S(1)} %add_compare_fusion.2), kind=kLoop, calls=%fused_computation.6.clone.1 | loop fusion | flops 10484736 | bytes 8398848 | tf_op jit(solution)/shard_map/while/body/eval_jaxpr/reduce_sum | solution.py:18
  81.8 5.1 %fusion.56 = bf16[64,2,8,128]{3,2,0,1:T(8,128)(2,1)S(1)} fusion(bf16[2048,2,128]{2,0,1:T(8,128)(2,1)S(1)} %get-tuple-element.221, f32[2,64,8,2048]{3,2,1,0:T(8,128)} %copy-done, f32[64,2,8]{2,0,1:T(8,128)S(1)} %get-tuple-element.197, pred[2048]{0:T(1024)(128)(4,1)S(1)} %add_compare_fusion.2, f32[64,2,8]{2,0,1:T(8,128)S(1)} %copy.142), kind=kOutput, calls=%fused_computation.16.clone.1 | convolution fusion | flops 547618816 | bytes 9709568 | tf_op jit(solution)/shard_map/while/body/eval_jaxpr/tkgs,skd->tkgd/dot_general | solution.py:19
  86.9 0.8 bitcast_dynamic-update-slice_fusion.4
  87.8 0.6 broadcast.66
  88.4 1.0 reduce
  89.4 0.7 reshape.128
  90.1 3.3 %all-to-all-start.1 = ((f32[4,1,1024]{2,1,0:T(1,128)}), f32[4,1,1024]{2,1,0:T(1,128)S(1)}, u32[]{:S(2)}, u32[]{:S(2)}) async-start(f32[4,1,1024]{2,1,0:T(1,128)} %reshape.128), calls=%async_computation.1 | async-start | bytes 32768 | tf_op jit(solution)/shard_map/all_to_all | solution.py:59
  93.4 0.4 convolution_bitcast_fusion
  93.8 3.4 %all-to-all-done.1 = f32[4,1,1024]{2,1,0:T(1,128)S(1)} async-done(((f32[4,1,1024]{2,1,0:T(1,128)}), f32[4,1,1024]{2,1,0:T(1,128)S(1)}, u32[]{:S(2)}, u32[]{:S(2)}) %all-to-all-start.1) | async-done | bytes 16416 | tf_op jit(solution)/shard_map/all_to_all | solution.py:59
  97.2 3.5 %all-to-all-start = ((bf16[1,256,16,128]{3,2,0,1:T(8,128)(2,1)}), bf16[1,256,16,128]{3,2,0,1:T(8,128)(2,1)S(1)}, u32[]{:S(2)}, u32[]{:S(2)}) async-start(bf16[1,256,16,128]{3,2,0,1:T(8,128)(2,1)} %bitcast.2), calls=%async_computation | async-start | bytes 2097152 | tf_op jit(solution)/shard_map/all_to_all | solution.py:58
  100.7 0.7 reduce.1
  101.4 0.2 reshape.129
  102.2 0.7 copy.114
  102.9 12.2 %all-to-all-done = bf16[1,256,16,128]{3,2,0,1:T(8,128)(2,1)S(1)} async-done(((bf16[1,256,16,128]{3,2,0,1:T(8,128)(2,1)}), bf16[1,256,16,128]{3,2,0,1:T(8,128)(2,1)S(1)}, u32[]{:S(2)}, u32[]{:S(2)}) %all-to-all-start) | async-done | bytes 1048608 | tf_op jit(solution)/shard_map/all_to_all | solution.py:58
  115.1 1.3 %fusion.31 = f32[64,16,1,128]{3,2,1,0:T(1,128)S(1)} fusion(bf16[4,64,16,1]{0,3,2,1:T(2,128)(2,1)S(1)} %copy.114, bf16[4,64,16,128]{3,2,1,0:T(8,128)(2,1)S(1)} %bitcast.123), kind=kOutput, calls=%fused_computation.31 | convolution fusion | flops 1048576 | bytes 1581056 | tf_op jit(solution)/shard_map/sthd,sth->thd/dot_general | solution.py:62
  116.4 1.1 fusion.37
  (40 shorter events, 1.6 us)
Async XLA Ops:
  6.5 22.5 %all-gather.2.cloned.1.call-start = ((), (), s32[]{:S(2)}) async-start(), calls=%async_computation.2 | async-start | bytes 1310720 | tf_op jit(solution)/shard_map/all_gather | solution.py:32
  32.1 3.2 %copy-start = (f32[2,64,8,2048]{3,2,1,0:T(8,128)}, f32[2,64,8,2048]{3,2,1,0:T(8,128)S(1)}, u32[]{:S(2)}) copy-start(f32[2,64,8,2048]{3,2,1,0:T(8,128)S(1)} %get-tuple-element.196) | copy-start | bytes 25165828 | tf_op jit(solution)/shard_map/while
  46.8 3.2 %copy-start = (f32[2,64,8,2048]{3,2,1,0:T(8,128)}, f32[2,64,8,2048]{3,2,1,0:T(8,128)S(1)}, u32[]{:S(2)}) copy-start(f32[2,64,8,2048]{3,2,1,0:T(8,128)S(1)} %get-tuple-element.196) | copy-start | bytes 25165828 | tf_op jit(solution)/shard_map/while
  61.4 3.2 %copy-start = (f32[2,64,8,2048]{3,2,1,0:T(8,128)}, f32[2,64,8,2048]{3,2,1,0:T(8,128)S(1)}, u32[]{:S(2)}) copy-start(f32[2,64,8,2048]{3,2,1,0:T(8,128)S(1)} %get-tuple-element.196) | copy-start | bytes 25165828 | tf_op jit(solution)/shard_map/while
  76.1 3.2 %copy-start = (f32[2,64,8,2048]{3,2,1,0:T(8,128)}, f32[2,64,8,2048]{3,2,1,0:T(8,128)S(1)}, u32[]{:S(2)}) copy-start(f32[2,64,8,2048]{3,2,1,0:T(8,128)S(1)} %get-tuple-element.196) | copy-start | bytes 25165828 | tf_op jit(solution)/shard_map/while
  90.1 7.1 %all-to-all-start.1 = ((f32[4,1,1024]{2,1,0:T(1,128)}), f32[4,1,1024]{2,1,0:T(1,128)S(1)}, u32[]{:S(2)}, u32[]{:S(2)}) async-start(f32[4,1,1024]{2,1,0:T(1,128)} %reshape.128), calls=%async_computation.1 | async-start | bytes 32768 | tf_op jit(solution)/shard_map/all_to_all | solution.py:59
  97.2 17.9 %all-to-all-start = ((bf16[1,256,16,128]{3,2,0,1:T(8,128)(2,1)}), bf16[1,256,16,128]{3,2,0,1:T(8,128)(2,1)S(1)}, u32[]{:S(2)}, u32[]{:S(2)}) async-start(bf16[1,256,16,128]{3,2,0,1:T(8,128)(2,1)} %bitcast.2), calls=%async_computation | async-start | bytes 2097152 | tf_op jit(solution)/shard_map/all_to_all | solution.py:58
Sparse Core Ops, SparseCore 0:
  8.9 20.1 all-gather.1
where the time goes:
time: 125 us; the launch traced here: 124 us
  matrix products  33.2 us (27%)
  local copies, waits for them, and re-layouts  23.8 us (19%)
  waiting for transfers between devices  19.2 us (15%)
  other arithmetic  14.9 us (12%)
  between operations  13.5 us (11%)
  blocking collectives  12.8 us (10%)
  starting transfers between devices  6.77 us (5%)
    dot_general x5, matrix products, attend_block(): jnp.einsum('tkgs,skd->tkgd', expo.astype(jnp.bfloat16), values, preferred...  20.8 us
    while x8, local copies, waits for them, and re-layouts  12.9 us
    all_to_all x1, waiting for transfers between devices, per_device(): lax.all_to_all(norm[None], 'ctx', split_axis=1, concat_axis=0, tiled=True)  12.2 us
    dot_general x5, matrix products, attend_block(): jnp.einsum('tkgd,skd->tkgs', query_rows, keys, preferred_element_type=jnp...  11 us
    reduce_sum x5, other arithmetic, attend_block(): total = jnp.sum(expo, axis=-1)  9.28 us
    all_gather x1, blocking collectives, per_device(): lax.all_gather(new_keys, 'ctx', axis=0, tiled=True)  6.49 us
    all_gather x1, blocking collectives, per_device(): lax.all_gather(new_values, 'ctx', axis=0, tiled=True)  6.3 us
    unnamed x7, local copies, waits for them, and re-layouts  5.81 us
  transfers between devices with their start and end apart: 3, of which 3 were waited for; matrix products, arithmetic and copies ran while one was open for 7% of the time, Pallas kernels for 0%

commit v1 on v0

--- a/solution.py
+++ b/solution.py
@@ -5,6 +5,23 @@
 from jax.sharding import PartitionSpec as P
 
 NEG_FILL = -1e30
+
+
+def find_tables(patch):
+    comm_axis = "ctx"
+    newest, o_now = (lax.psum(1, comm_axis), lax.axis_index(comm_axis))
+    y_new = patch.shape[1] // newest
+    kept_arr = jnp.roll(patch, -o_now * y_new, axis=1)
+    found = [lax.slice_in_dim(kept_arr, 0, y_new, axis=1)]
+    to_i = 1
+    while to_i < newest:
+        known = lax.slice_in_dim(kept_arr, to_i * y_new, (to_i + 1) * y_new, axis=1)
+        found.append(
+            lax.ppermute(known, comm_axis, [(m, (m + to_i) % newest) for m in range(newest)])
+        )
+        to_i = to_i + 1
+    last = jnp.concatenate(found[::-1], axis=0)
+    return jnp.roll(last, (o_now + 1) * found[0].shape[0], axis=0)
 
 
 def attend_block(query_rows, keys, values, valid):
@@ -56,7 +73,7 @@
     turn_max = turn_max.reshape(q_rows, heads_local)
     turn_total = turn_total.reshape(q_rows, heads_local)
     got_norm = lax.all_to_all(norm[None], "ctx", split_axis=1, concat_axis=0, tiled=True)
-    got_lse = lax.all_to_all(lse[None], "ctx", split_axis=1, concat_axis=0, tiled=True)
+    got_lse = find_tables(lse[None])
     top = jnp.maximum(jnp.max(got_lse, axis=0), turn_max)
     shard_scale = jnp.exp(got_lse - top[None])
     numer = jnp.einsum("sthd,sth->thd", got_norm.astype(jnp.float32), shard_scale)

time: 125 us -> 118 us (0.944)
  waiting for transfers between devices: 19.2 us -> 17 us
  other arithmetic: 14.9 us -> 13.2 us
  local copies, waits for them, and re-layouts: 23.8 us -> 22.2 us
  starting transfers between devices: 6.77 us -> 5.46 us
    all_to_all x1 -> x0, waiting for transfers between devices: 3.42 us -> none  [per_device(): lax.all_to_all(lse[None], 'ctx', split_axis=1, concat_axis=0, tiled=True)]
    all_to_all x1 -> x0, starting transfers between devices: 3.25 us -> none  [per_device(): lax.all_to_all(lse[None], 'ctx', split_axis=1, concat_axis=0, tiled=True)]
    ppermute x0 -> x3, starting transfers between devices: none -> 1.94 us  [find_tables(): lax.ppermute(known, comm_axis, [(m, (m + to_i) % newest) for m in range(n...]
    unnamed x7 -> x11, local copies, waits for them, and re-layouts: 5.81 us -> 4.28 us
    dynamic_update_slice x4 -> x8, local copies, waits for them, and re-layouts: 3.06 us -> 3.27 us  [per_device(): norm, lse = lax.map(one_block, blocks)]
  transfers between devices with their start and end apart: 3 -> 5, of which waited for: 3 -> 2; matrix products, arithmetic and copies ran while one was open for 7% -> 6% of each run, Pallas kernels for 0% -> 0%
where the time goes in v1:
time: 118 us
  matrix products  33.1 us (28%)
  local copies, waits for them, and re-layouts  22.2 us (19%)
  waiting for transfers between devices  17 us (14%)
  between operations  13.6 us (12%)
  other arithmetic  13.2 us (11%)
  blocking collectives  12.8 us (11%)
  starting transfers between devices  5.46 us (5%)
    dot_general x5, matrix products, attend_block(): jnp.einsum('tkgs,skd->tkgd', expo.astype(jnp.bfloat16), values, preferred...  20.8 us
    all_to_all x1, waiting for transfers between devices, per_device(): lax.all_to_all(norm[None], 'ctx', split_axis=1, concat_axis=0, tiled=True)  13.4 us
    while x8, local copies, waits for them, and re-layouts  12.9 us
    dot_general x5, matrix products, attend_block(): jnp.einsum('tkgd,skd->tkgs', query_rows, keys, preferred_element_type=jnp...  11 us
    reduce_sum x5, other arithmetic, attend_block(): total = jnp.sum(expo, axis=-1)  9.25 us
    all_gather x1, blocking collectives, per_device(): lax.all_gather(new_keys, 'ctx', axis=0, tiled=True)  6.49 us
    all_gather x1, blocking collectives, per_device(): lax.all_gather(new_values, 'ctx', axis=0, tiled=True)  6.31 us
    unnamed x11, local copies, waits for them, and re-layouts  4.28 us
  transfers between devices with their start and end apart: 5, of which 2 were waited for; matrix products, arithmetic and copies ran while one was open for 6% of the time, Pallas kernels for 0%

profile of v1, /device:TPU:0, one launch (start us, length us, event | category | flops | bytes accessed | tf_op | source)
XLA Modules:
  0.0 117.6 jit_solution(12209949692334802555)
XLA Ops:
  6.5 0.7 all-gather.2.cloned.1.call-update
  7.3 1.4 %copy.61 = bf16[2048,2,128]{2,0,1:T(8,128)(2,1)S(1)} copy(bf16[2048,2,128]{2,1,0:T(2,128)(2,1)} %param.11) | data formatting | bytes 2097152
  8.7 1.4 %copy.62 = bf16[2048,2,128]{2,0,1:T(8,128)(2,1)S(1)} copy(bf16[2048,2,128]{2,1,0:T(2,128)(2,1)} %param.12) | data formatting | bytes 2097152
  10.0 0.8 copy.64
  10.8 0.8 copy.66
  11.6 6.5 %all_gather.10 = bf16[256,2,128]{2,0,1:T(8,128)(2,1)S(1)} all-gather(bf16[64,2,128]{2,0,1:T(8,128)(2,1)S(1)} %copy.64), channel_id=1, replica_groups=mesh['conv'=2,'ctx'=4,'head'=4] {'ctx'}, dimensions={0}, use_global_device_ids=true | all-gather | bytes 163840 | tf_op jit(solution)/shard_map/all_gather | solution.py:64
  18.1 6.3 %all_gather.11 = bf16[256,2,128]{2,0,1:T(8,128)(2,1)S(1)} all-gather(bf16[64,2,128]{2,0,1:T(8,128)(2,1)S(1)} %copy.66), channel_id=1, replica_groups=mesh['conv'=2,'ctx'=4,'head'=4] {'ctx'}, dimensions={0}, use_global_device_ids=true | all-gather | bytes 163840 | tf_op jit(solution)/shard_map/all_gather | solution.py:65
  24.5 1.3 %fusion.49 = (f32[64,2,8]{0,2,1:T(8,128)S(1)}, f32[64,2,8,256]{3,0,2,1:T(8,128)S(1)}) fusion(bf16[64,2,8,128]{3,2,1,0:T(8,128)(2,1)} %bitcast.121, bf16[256,2,128]{2,0,1:T(8,128)(2,1)S(1)} %all_gather.10, pred[64,256]{1,0:T(8,128)(4,1)S(1)} %iota_compare_fusion), kind=kOutput, calls=%fused_computation.66 | convolution fusion | flops 67894272 | bytes 1462272 | tf_op jit(solution)/shard_map/tkgd,skd->tkgs/dot_general | solution.py:28
  25.8 0.4 fusion.33
  26.2 2.8 %all-gather.2.cloned.1.call-done = bf16[256,16,128]{2,1,0:T(8,128)(2,1)} async-done(((bf16[64,16,128]{2,1,0:T(8,128)(2,1)}), bf16[256,16,128]{2,1,0:T(8,128)(2,1)}) %all-gather.2.cloned.1.call-update) | async-done | bytes 1048592 | tf_op jit(solution)/shard_map/all_gather | solution.py:49
  29.0 58.8 %while.13 = (s32[]{:T(128)}, bf16[4,64,16,128]{3,2,1,0:T(8,128)(2,1)}, f32[4,64,16]{1,0,2:T(4,128)S(1)}, bf16[4,64,2,8,128]{4,3,2,1,0:T(8,128)(2,1)}, bf16[2048,...) while((s32[]{:T(128)}, ...), condition=%wide.region_3.4_spmd.clone, body=%wide.region_0.3_spmd.clone.sunk | while | flops 1101271040 | bytes 61944972 | solution.py:61
  29.0 0.7 add_compare_fusion.2
  29.7 2.4 %bitcast_reduce_fusion.2 = (f32[64,2,8]{2,0,1:T(8,128)S(1)}, f32[2,64,8,2048]{3,2,1,0:T(8,128)S(1)}) fusion(pred[2048]{0:T(1024)(128)(4,1)S(1)} %add_compare_fusion.2, bf16[2048,2,128]{2,0,1:T(8,128)(2,1)S(1)} %get-tuple-element.215, bf16[4,64,2,8,128]{4,3,2,1,0:T(8,128)(2,1)} %get-tuple-element.214, s32[]{:T(128)} %get-tuple-element.201), kind=kOutput, calls=%fused_computation.2.clone.1 | convolution fusion | flops 543161344 | bytes 9705984 | tf_op jit(solution)/shard_map/while/body/eval_jaxpr/tkgd,skd->tkgs/dot_general | solution.py:28
  32.1 3.2 %copy-done = f32[2,64,8,2048]{3,2,1,0:T(8,128)} copy-done((f32[2,64,8,2048]{3,2,1,0:T(8,128)}, f32[2,64,8,2048]{3,2,1,0:T(8,128)S(1)}, u32[]{:S(2)}) %copy-start) | copy-done | bytes 8388632 | tf_op jit(solution)/shard_map/while
  35.4 2.2 %fusion.57 = f32[64,2,8]{2,0,1:T(8,128)S(1)} fusion(f32[2,64,8,2048]{3,2,1,0:T(8,128)S(1)} %get-tuple-element.187, f32[64,2,8]{2,0,1:T(8,128)S(1)} %get-tuple-element.188, pred[2048]{0:T(1024)(128)(4,1)S(1)} %add_compare_fusion.2), kind=kLoop, calls=%fused_computation.6.clone.1 | loop fusion | flops 10484736 | bytes 8398848 | tf_op jit(solution)/shard_map/while/body/eval_jaxpr/reduce_sum | solution.py:35
  37.7 0.1 copy.106
  37.8 5.1 %fusion.58 = bf16[64,2,8,128]{3,2,0,1:T(8,128)(2,1)S(1)} fusion(bf16[2048,2,128]{2,0,1:T(8,128)(2,1)S(1)} %get-tuple-element.216, f32[2,64,8,2048]{3,2,1,0:T(8,128)} %copy-done, f32[64,2,8]{2,0,1:T(8,128)S(1)} %get-tuple-element.188, pred[2048]{0:T(1024)(128)(4,1)S(1)} %add_compare_fusion.2, f32[64,2,8]{2,0,1:T(8,128)S(1)} %copy.106), kind=kOutput, calls=%fused_computation.16.clone.1 | convolution fusion | flops 547618816 | bytes 9709568 | tf_op jit(solution)/shard_map/while/body/eval_jaxpr/tkgs,skd->tkgd/dot_general | solution.py:36
  42.9 0.8 bitcast_dynamic-update-slice_fusion.2
  43.7 0.7 add_compare_fusion.2
  44.4 2.4 %bitcast_reduce_fusion.2 = (f32[64,2,8]{2,0,1:T(8,128)S(1)}, f32[2,64,8,2048]{3,2,1,0:T(8,128)S(1)}) fusion(pred[2048]{0:T(1024)(128)(4,1)S(1)} %add_compare_fusion.2, bf16[2048,2,128]{2,0,1:T(8,128)(2,1)S(1)} %get-tuple-element.215, bf16[4,64,2,8,128]{4,3,2,1,0:T(8,128)(2,1)} %get-tuple-element.214, s32[]{:T(128)} %get-tuple-element.201), kind=kOutput, calls=%fused_computation.2.clone.1 | convolution fusion | flops 543161344 | bytes 9705984 | tf_op jit(solution)/shard_map/while/body/eval_jaxpr/tkgd,skd->tkgs/dot_general | solution.py:28
  46.8 3.2 %copy-done = f32[2,64,8,2048]{3,2,1,0:T(8,128)} copy-done((f32[2,64,8,2048]{3,2,1,0:T(8,128)}, f32[2,64,8,2048]{3,2,1,0:T(8,128)S(1)}, u32[]{:S(2)}) %copy-start) | copy-done | bytes 8388632 | tf_op jit(solution)/shard_map/while
  50.0 2.2 %fusion.57 = f32[64,2,8]{2,0,1:T(8,128)S(1)} fusion(f32[2,64,8,2048]{3,2,1,0:T(8,128)S(1)} %get-tuple-element.187, f32[64,2,8]{2,0,1:T(8,128)S(1)} %get-tuple-element.188, pred[2048]{0:T(1024)(128)(4,1)S(1)} %add_compare_fusion.2), kind=kLoop, calls=%fused_computation.6.clone.1 | loop fusion | flops 10484736 | bytes 8398848 | tf_op jit(solution)/shard_map/while/body/eval_jaxpr/reduce_sum | solution.py:35
  52.4 0.1 copy.106
  52.5 5.1 %fusion.58 = bf16[64,2,8,128]{3,2,0,1:T(8,128)(2,1)S(1)} fusion(bf16[2048,2,128]{2,0,1:T(8,128)(2,1)S(1)} %get-tuple-element.216, f32[2,64,8,2048]{3,2,1,0:T(8,128)} %copy-done, f32[64,2,8]{2,0,1:T(8,128)S(1)} %get-tuple-element.188, pred[2048]{0:T(1024)(128)(4,1)S(1)} %add_compare_fusion.2, f32[64,2,8]{2,0,1:T(8,128)S(1)} %copy.106), kind=kOutput, calls=%fused_computation.16.clone.1 | convolution fusion | flops 547618816 | bytes 9709568 | tf_op jit(solution)/shard_map/while/body/eval_jaxpr/tkgs,skd->tkgd/dot_general | solution.py:36
  57.6 0.8 bitcast_dynamic-update-slice_fusion.2
  58.4 0.7 add_compare_fusion.2
  59.1 2.4 %bitcast_reduce_fusion.2 = (f32[64,2,8]{2,0,1:T(8,128)S(1)}, f32[2,64,8,2048]{3,2,1,0:T(8,128)S(1)}) fusion(pred[2048]{0:T(1024)(128)(4,1)S(1)} %add_compare_fusion.2, bf16[2048,2,128]{2,0,1:T(8,128)(2,1)S(1)} %get-tuple-element.215, bf16[4,64,2,8,128]{4,3,2,1,0:T(8,128)(2,1)} %get-tuple-element.214, s32[]{:T(128)} %get-tuple-element.201), kind=kOutput, calls=%fused_computation.2.clone.1 | convolution fusion | flops 543161344 | bytes 9705984 | tf_op jit(solution)/shard_map/while/body/eval_jaxpr/tkgd,skd->tkgs/dot_general | solution.py:28
  61.5 3.2 %copy-done = f32[2,64,8,2048]{3,2,1,0:T(8,128)} copy-done((f32[2,64,8,2048]{3,2,1,0:T(8,128)}, f32[2,64,8,2048]{3,2,1,0:T(8,128)S(1)}, u32[]{:S(2)}) %copy-start) | copy-done | bytes 8388632 | tf_op jit(solution)/shard_map/while
  64.7 2.2 %fusion.57 = f32[64,2,8]{2,0,1:T(8,128)S(1)} fusion(f32[2,64,8,2048]{3,2,1,0:T(8,128)S(1)} %get-tuple-element.187, f32[64,2,8]{2,0,1:T(8,128)S(1)} %get-tuple-element.188, pred[2048]{0:T(1024)(128)(4,1)S(1)} %add_compare_fusion.2), kind=kLoop, calls=%fused_computation.6.clone.1 | loop fusion | flops 10484736 | bytes 8398848 | tf_op jit(solution)/shard_map/while/body/eval_jaxpr/reduce_sum | solution.py:35
  67.1 0.1 copy.106
  67.2 5.1 %fusion.58 = bf16[64,2,8,128]{3,2,0,1:T(8,128)(2,1)S(1)} fusion(bf16[2048,2,128]{2,0,1:T(8,128)(2,1)S(1)} %get-tuple-element.216, f32[2,64,8,2048]{3,2,1,0:T(8,128)} %copy-done, f32[64,2,8]{2,0,1:T(8,128)S(1)} %get-tuple-element.188, pred[2048]{0:T(1024)(128)(4,1)S(1)} %add_compare_fusion.2, f32[64,2,8]{2,0,1:T(8,128)S(1)} %copy.106), kind=kOutput, calls=%fused_computation.16.clone.1 | convolution fusion | flops 547618816 | bytes 9709568 | tf_op jit(solution)/shard_map/while/body/eval_jaxpr/tkgs,skd->tkgd/dot_general | solution.py:36
  72.3 0.8 bitcast_dynamic-update-slice_fusion.2
  73.1 0.7 add_compare_fusion.2
  73.8 2.4 %bitcast_reduce_fusion.2 = (f32[64,2,8]{2,0,1:T(8,128)S(1)}, f32[2,64,8,2048]{3,2,1,0:T(8,128)S(1)}) fusion(pred[2048]{0:T(1024)(128)(4,1)S(1)} %add_compare_fusion.2, bf16[2048,2,128]{2,0,1:T(8,128)(2,1)S(1)} %get-tuple-element.215, bf16[4,64,2,8,128]{4,3,2,1,0:T(8,128)(2,1)} %get-tuple-element.214, s32[]{:T(128)} %get-tuple-element.201), kind=kOutput, calls=%fused_computation.2.clone.1 | convolution fusion | flops 543161344 | bytes 9705984 | tf_op jit(solution)/shard_map/while/body/eval_jaxpr/tkgd,skd->tkgs/dot_general | solution.py:28
  76.2 3.2 %copy-done = f32[2,64,8,2048]{3,2,1,0:T(8,128)} copy-done((f32[2,64,8,2048]{3,2,1,0:T(8,128)}, f32[2,64,8,2048]{3,2,1,0:T(8,128)S(1)}, u32[]{:S(2)}) %copy-start) | copy-done | bytes 8388632 | tf_op jit(solution)/shard_map/while
  79.4 2.2 %fusion.57 = f32[64,2,8]{2,0,1:T(8,128)S(1)} fusion(f32[2,64,8,2048]{3,2,1,0:T(8,128)S(1)} %get-tuple-element.187, f32[64,2,8]{2,0,1:T(8,128)S(1)} %get-tuple-element.188, pred[2048]{0:T(1024)(128)(4,1)S(1)} %add_compare_fusion.2), kind=kLoop, calls=%fused_computation.6.clone.1 | loop fusion | flops 10484736 | bytes 8398848 | tf_op jit(solution)/shard_map/while/body/eval_jaxpr/reduce_sum | solution.py:35
  81.8 0.1 copy.106
  81.9 5.1 %fusion.58 = bf16[64,2,8,128]{3,2,0,1:T(8,128)(2,1)S(1)} fusion(bf16[2048,2,128]{2,0,1:T(8,128)(2,1)S(1)} %get-tuple-element.216, f32[2,64,8,2048]{3,2,1,0:T(8,128)} %copy-done, f32[64,2,8]{2,0,1:T(8,128)S(1)} %get-tuple-element.188, pred[2048]{0:T(1024)(128)(4,1)S(1)} %add_compare_fusion.2, f32[64,2,8]{2,0,1:T(8,128)S(1)} %copy.106), kind=kOutput, calls=%fused_computation.16.clone.1 | convolution fusion | flops 547618816 | bytes 9709568 | tf_op jit(solution)/shard_map/while/body/eval_jaxpr/tkgs,skd->tkgd/dot_general | solution.py:36
  87.0 0.8 bitcast_dynamic-update-slice_fusion.2
  87.8 0.1 broadcast_in_dim_reshape.7
  88.1 0.2 collective-permute-start
  88.3 0.4 convolution_bitcast_fusion
  88.7 1.7 %collective-permute-start.1 = (f32[1,64,16]{1,2,0:T(8,128)S(1)}, f32[1,64,16]{1,2,0:T(8,128)S(1)}, u32[]{:S(2)}, u32[]{:S(2)}) collective-permute-start(f32[1,64,16]{1,2,0:T(8,128)S(1)} %get-tuple-element.130), channel_id=1, source_target_pairs={{0,8},{4,12},{8,0},{12,4},{1,9},{5,13},{9,1},{13,5},{2,10},{6,14},... | collective-permute-start | bytes 12296 | tf_op jit(solution)/shard_map/ppermute | solution.py:20
  90.4 3.5 %all-to-all-start = ((bf16[1,256,16,128]{3,2,0,1:T(8,128)(2,1)}), bf16[1,256,16,128]{3,2,0,1:T(8,128)(2,1)S(1)}, u32[]{:S(2)}, u32[]{:S(2)}) async-start(bf16[1,256,16,128]{3,2,0,1:T(8,128)(2,1)} %bitcast.120), calls=%async_computation | async-start | bytes 2097152 | tf_op jit(solution)/shard_map/all_to_all | solution.py:75
  94.3 0.6 copy.75
  94.9 13.4 %all-to-all-done = bf16[1,256,16,128]{3,2,0,1:T(8,128)(2,1)S(1)} async-done(((bf16[1,256,16,128]{3,2,0,1:T(8,128)(2,1)}), bf16[1,256,16,128]{3,2,0,1:T(8,128)(2,1)S(1)}, u32[]{:S(2)}, u32[]{:S(2)}) %all-to-all-start) | async-done | bytes 1048608 | tf_op jit(solution)/shard_map/all_to_all | solution.py:75
  108.3 1.3 %fusion.31 = f32[64,16,1,128]{3,2,1,0:T(1,128)S(1)} fusion(bf16[4,64,16,1]{0,3,2,1:T(2,128)(2,1)S(1)} %copy.75, bf16[4,64,16,128]{3,2,1,0:T(8,128)(2,1)S(1)} %bitcast.119), kind=kOutput, calls=%fused_computation.31 | convolution fusion | flops 1048576 | bytes 1581056 | tf_op jit(solution)/shard_map/sthd,sth->thd/dot_general | solution.py:79
  109.7 1.1 fusion.37
  (46 shorter events, 1.3 us)
Async XLA Ops:
  6.5 22.5 %all-gather.2.cloned.1.call-start = ((), (), s32[]{:S(2)}) async-start(), calls=%async_computation.1 | async-start | bytes 1310720 | tf_op jit(solution)/shard_map/all_gather | solution.py:49
  32.1 3.2 %copy-start = (f32[2,64,8,2048]{3,2,1,0:T(8,128)}, f32[2,64,8,2048]{3,2,1,0:T(8,128)S(1)}, u32[]{:S(2)}) copy-start(f32[2,64,8,2048]{3,2,1,0:T(8,128)S(1)} %get-tuple-element.187) | copy-start | bytes 25165828 | tf_op jit(solution)/shard_map/while
  46.8 3.2 %copy-start = (f32[2,64,8,2048]{3,2,1,0:T(8,128)}, f32[2,64,8,2048]{3,2,1,0:T(8,128)S(1)}, u32[]{:S(2)}) copy-start(f32[2,64,8,2048]{3,2,1,0:T(8,128)S(1)} %get-tuple-element.187) | copy-start | bytes 25165828 | tf_op jit(solution)/shard_map/while
  61.5 3.2 %copy-start = (f32[2,64,8,2048]{3,2,1,0:T(8,128)}, f32[2,64,8,2048]{3,2,1,0:T(8,128)S(1)}, u32[]{:S(2)}) copy-start(f32[2,64,8,2048]{3,2,1,0:T(8,128)S(1)} %get-tuple-element.187) | copy-start | bytes 25165828 | tf_op jit(solution)/shard_map/while
  76.2 3.2 %copy-start = (f32[2,64,8,2048]{3,2,1,0:T(8,128)}, f32[2,64,8,2048]{3,2,1,0:T(8,128)S(1)}, u32[]{:S(2)}) copy-start(f32[2,64,8,2048]{3,2,1,0:T(8,128)S(1)} %get-tuple-element.187) | copy-start | bytes 25165828 | tf_op jit(solution)/shard_map/while
  88.1 5.9 %collective-permute-start = (f32[1,64,16]{1,2,0:T(8,128)S(1)}, f32[1,64,16]{1,2,0:T(8,128)S(1)}, u32[]{:S(2)}, u32[]{:S(2)}) collective-permute-start(f32[1,64,16]{1,2,0:T(8,128)S(1)} %get-tuple-element.131), channel_id=1, source_target_pairs={{0,12},{4,0},{8,4},{12,8},{1,13},{5,1},{9,5},{13,9},{2,14},{6,2},{... | collective-permute-start | bytes 12296 | tf_op jit(solution)/shard_map/ppermute | solution.py:20
  88.7 5.3 %collective-permute-start.1 = (f32[1,64,16]{1,2,0:T(8,128)S(1)}, f32[1,64,16]{1,2,0:T(8,128)S(1)}, u32[]{:S(2)}, u32[]{:S(2)}) collective-permute-start(f32[1,64,16]{1,2,0:T(8,128)S(1)} %get-tuple-element.130), channel_id=1, source_target_pairs={{0,8},{4,12},{8,0},{12,4},{1,9},{5,13},{9,1},{13,5},{2,10},{6,14},... | collective-permute-start | bytes 12296 | tf_op jit(solution)/shard_map/ppermute | solution.py:20
  90.4 3.6 %collective-permute-start.2 = (f32[1,64,16]{1,2,0:T(8,128)S(1)}, f32[1,64,16]{1,2,0:T(8,128)S(1)}, u32[]{:S(2)}, u32[]{:S(2)}) collective-permute-start(f32[1,64,16]{1,2,0:T(8,128)S(1)} %get-tuple-element.129), channel_id=1, source_target_pairs={{0,4},{4,8},{8,12},{12,0},{1,5},{5,9},{9,13},{13,1},{2,6},{6,10},{... | collective-permute-start | bytes 12296 | tf_op jit(solution)/shard_map/ppermute | solution.py:20
  90.4 17.9 %all-to-all-start = ((bf16[1,256,16,128]{3,2,0,1:T(8,128)(2,1)}), bf16[1,256,16,128]{3,2,0,1:T(8,128)(2,1)S(1)}, u32[]{:S(2)}, u32[]{:S(2)}) async-start(bf16[1,256,16,128]{3,2,0,1:T(8,128)(2,1)} %bitcast.120), calls=%async_computation | async-start | bytes 2097152 | tf_op jit(solution)/shard_map/all_to_all | solution.py:75
Sparse Core Ops, SparseCore 0:
  8.9 20.1 all-gather.1
